TPU v7x, 256 devices: a whole 4x4x8 slice. The times are simulated.
256 devices in a mesh: pipe: 4 (over y), expert: 16 (over z, core), dp: 4 (over x).
Axes of the slice: x: 4, y: 4, z: 8, core: 2. Of those that a mesh axis runs over, the one named last changes fastest.
Arguments:
- normed: bfloat16 [4, 4, 3072, 4096], P('pipe', None, ('expert', 'dp')), may hold values from -1.5 to 1.5
- saved_out: bfloat16 [4, 4, 3072, 2, 4096], P('pipe', None, ('expert', 'dp')), may hold values from -0.59765625 to 0.59765625
- expert_grads: bfloat16 [4, 4, 4, 16, 16, 9, 4096], P('pipe', None, 'dp', 'expert'), may hold values from -24 to 24
- routes: int32 [4, 4, 3072, 2], P('pipe', None, ('expert', 'dp')), may hold values from 0 to 15, all different within a row; in each aligned block of 48 rows (0 to 47, 48 to 95, ..., all dimensions but the last counted through in order) at most 9 rows name the same one
- router_weight: bfloat16 [4, 4096, 16], P('pipe'), may hold values from -0.375 to 0.375
- upstream: bfloat16 [4, 3072, 4096], P(None, ('expert', 'dp')), may hold values from -6 to 6
Outputs:
- grad_input: bfloat16 [4, 4, 3072, 4096], P('pipe', None, ('expert', 'dp'))
- router_grad: float32 [4, 4096, 16], P('pipe')
Inputs may be any that keep to these rules, and one draw needn't show every extreme that they name: `routes`: the two experts of a row differ. Within the 48 rows of one device for one section and micro-batch no expert is named more than 9 times, a bound that some expert reaches in some of these blocks.
All inputs are finite; a program needn't handle non-finite values.
Results may differ from a plain program's by a relative error of at most 0.007.
Values may be sent and summed in bfloat16 or wider, within the bound.
No kernel may reach another device: no remote copies, remote signals or barrier semaphores. Data moves between devices by JAX's collectives and lax.ppermute only.
A program may use at most 128 MiB of HBM per device.

v0:
```python
import jax
import jax.numpy as jnp
from jax import lax
from jax.sharding import PartitionSpec as P


def shifted(block, axis, distance):
    devices = range(lax.axis_size(axis))
    route = [(i - distance, i) for i in devices if i - distance in devices]
    return lax.ppermute(block, axis, route)


def slot_index(flat, experts, capacity):
    onehot = (flat[..., None] == jnp.arange(experts, dtype=jnp.int32)).astype(jnp.int32)
    before = jnp.cumsum(onehot, axis=-2) - onehot
    position = jnp.sum(before * onehot, axis=-1)
    return flat * capacity + position


def block_grad(incoming, normed_rows, saved_rows, route_rows, returned, index_rows, router_w):
    experts = router_w.shape[1]
    rows_dev = normed_rows.shape[0]
    width = normed_rows.shape[1]
    logits = jnp.dot(normed_rows, router_w, preferred_element_type=jnp.float32)
    expl = jnp.exp(logits)
    probs = expl / jnp.sum(expl, axis=-1, keepdims=True)
    chosen = (route_rows[..., None] == jnp.arange(experts, dtype=jnp.int32)).astype(jnp.float32)
    gates = jnp.einsum("tke,te->tk", chosen, probs)
    dot_grads = jnp.einsum("td,tkd->tk", incoming, saved_rows, preferred_element_type=jnp.float32)
    weighted = dot_grads * gates
    dense_f = (
        jnp.einsum("tke,tk->te", chosen, weighted) - probs * jnp.sum(weighted, axis=-1)[:, None]
    )
    dense = dense_f.astype(jnp.bfloat16)
    router_term = lax.dot_general(
        dense, router_w, (((1,), (1,)), ((), ())), preferred_element_type=jnp.float32
    )
    back_rows = returned[index_rows].reshape(rows_dev, 2, width).astype(jnp.float32)
    total = (
        incoming.astype(jnp.float32)
        + gates[:, 0, None] * back_rows[:, 0]
        + gates[:, 1, None] * back_rows[:, 1]
        + router_term
    )
    weight_part = lax.dot_general(
        normed_rows, dense, (((0,), (0,)), ((), ())), preferred_element_type=jnp.float32
    )
    return (total.astype(jnp.bfloat16), weight_part)


def on_device(normed, saved_out, expert_grads, routes, router_weight, upstream):
    micro = normed.shape[1]
    rows_dev = normed.shape[2]
    width = normed.shape[3]
    sections = lax.axis_size("pipe")
    section_idx = lax.axis_index("pipe")
    router_w = router_weight[0]
    experts = router_w.shape[1]
    capacity = expert_grads.shape[5]
    slot_rows = slot_index(routes[0].reshape(micro, -1), experts, capacity)
    local_grads = expert_grads[0, :, 0]
    returned_list = []
    for block_num in range(micro):
        received = lax.all_to_all(
            local_grads[block_num], "expert", split_axis=1, concat_axis=0, tiled=True
        )
        returned_list.append(received.reshape(experts * capacity, width))
    returned_all = jnp.stack(returned_list)
    grad_buffer = jnp.zeros((micro, rows_dev, width), jnp.bfloat16)
    weight_sum = jnp.zeros((width, experts), jnp.float32)
    passed = jnp.zeros((rows_dev, width), jnp.bfloat16)
    for tick_num in range(micro + sections - 1):
        if tick_num > 0:
            passed = shifted(passed, "pipe", -1)
        block_num = tick_num - (sections - 1 - section_idx)
        is_active = (block_num >= 0) & (block_num < micro)
        block_idx = jnp.clip(block_num, 0, micro - 1)
        returned = lax.dynamic_index_in_dim(returned_all, block_idx, 0, keepdims=False)
        from_top = lax.dynamic_index_in_dim(upstream, block_idx, 0, keepdims=False)
        incoming = jnp.where(section_idx == sections - 1, from_top, passed)
        new_grad, weight_part = block_grad(
            incoming,
            lax.dynamic_index_in_dim(normed[0], block_idx, 0, keepdims=False),
            lax.dynamic_index_in_dim(saved_out[0], block_idx, 0, keepdims=False),
            lax.dynamic_index_in_dim(routes[0], block_idx, 0, keepdims=False),
            returned,
            lax.dynamic_index_in_dim(slot_rows, block_idx, 0, keepdims=False),
            router_w,
        )
        updated = lax.dynamic_update_index_in_dim(grad_buffer, new_grad, block_idx, 0)
        grad_buffer = jnp.where(is_active, updated, grad_buffer)
        weight_sum = weight_sum + jnp.where(is_active, weight_part, 0.0)
        passed = new_grad
    router_grad = lax.psum(weight_sum / micro, ("expert", "dp"))
    return (grad_buffer[None], router_grad[None])


def solution(mesh):
    in_specs = (
        P("pipe", None, ("expert", "dp"), None),
        P("pipe", None, ("expert", "dp"), None, None),
        P("pipe", None, "dp", "expert", None, None, None),
        P("pipe", None, ("expert", "dp"), None),
        P("pipe", None, None),
        P(None, ("expert", "dp"), None),
    )
    out_specs = (P("pipe", None, ("expert", "dp"), None), P("pipe", None, None))
    return jax.shard_map(
        on_device, mesh=mesh, in_specs=in_specs, out_specs=out_specs, check_vma=False
    )
```

profile of v0, /device:TPU:1, one launch (start us, length us, event | category | flops | bytes accessed | tf_op | source)
XLA Modules:
  0.0 636.1 jit_solution(2353032965511129839)
XLA Ops:
  7.2 4.4 fusion.196
  11.6 2.1 copy.367
  13.7 10.1 %all-to-all-start = ((bf16[1,16,9,4096]{3,2,0,1:T(8,128)(2,1)}), bf16[1,16,9,4096]{3,2,0,1:T(8,128)(2,1)}, u32[]{:S(2)}, u32[]{:S(2)}) async-start(bf16[1,16,9,4096]{3,2,0,1:T(8,128)(2,1)} %bitcast.551), calls=%async_computation | async-start | bytes 4194304 | tf_op jit(solution)/shard_map/all_to_all | solution.py:64
  27.9 2.1 fusion.49
  30.8 3.4 copy.366
  39.4 33.5 %all-to-all-done = bf16[1,16,9,4096]{3,2,0,1:T(8,128)(2,1)} async-done(((bf16[1,16,9,4096]{3,2,0,1:T(8,128)(2,1)}), bf16[1,16,9,4096]{3,2,0,1:T(8,128)(2,1)}, u32[]{:S(2)}, u32[]{:S(2)}) %all-to-all-start) | async-done | bytes 1179680 | tf_op jit(solution)/shard_map/all_to_all | solution.py:64
  72.9 5.0 all-to-all-start.1
  78.8 3.5 copy.365
  82.3 2.1 copy.364
  97.5 29.4 %all-to-all-done.1 = bf16[1,16,9,4096]{3,2,0,1:T(8,128)(2,1)} async-done(((bf16[1,16,9,4096]{3,2,0,1:T(8,128)(2,1)}), bf16[1,16,9,4096]{3,2,0,1:T(8,128)(2,1)}, u32[]{:S(2)}, u32[]{:S(2)}) %all-to-all-start.1) | async-done | bytes 1179680 | tf_op jit(solution)/shard_map/all_to_all | solution.py:64
  126.9 5.0 all-to-all-start.2
  143.3 37.7 %all-to-all-done.2 = bf16[1,16,9,4096]{3,2,0,1:T(8,128)(2,1)} async-done(((bf16[1,16,9,4096]{3,2,0,1:T(8,128)(2,1)}), bf16[1,16,9,4096]{3,2,0,1:T(8,128)(2,1)}, u32[]{:S(2)}, u32[]{:S(2)}) %all-to-all-start.2) | async-done | bytes 1179680 | tf_op jit(solution)/shard_map/all_to_all | solution.py:64
  181.0 5.1 all-to-all-start.3
  188.2 2.6 stack_reshape.12
  190.8 2.7 stack_reshape.13
  193.5 2.6 stack_reshape.14
  196.1 2.5 constant_dynamic-update-slice_fusion.3
  201.4 33.7 %all-to-all-done.3 = bf16[1,16,9,4096]{3,2,0,1:T(8,128)(2,1)} async-done(((bf16[1,16,9,4096]{3,2,0,1:T(8,128)(2,1)}), bf16[1,16,9,4096]{3,2,0,1:T(8,128)(2,1)}, u32[]{:S(2)}, u32[]{:S(2)}) %all-to-all-start.3) | async-done | bytes 1179680 | tf_op jit(solution)/shard_map/all_to_all | solution.py:64
  235.1 2.6 stack_reshape.15
  237.8 2.4 constant_dynamic-update-slice_fusion
  240.2 7.0 %dynamic-slice_bitcast_fusion = (bf16[144,4096]{1,0:T(8,128)(2,1)}, bf16[144,4096]{1,0:T(8,128)(2,1)}, bf16[144,4096]{1,0:T(8,128)(2,1)}, bf16[144,4096]{1,0:T(8...) fusion(bf16[4,144,4096]{2,1,0:T(8,128)(2,1)} %constant_dynamic-update-slice_fusion, ...), kind=kLoop, calls=%fused_computation.28 | loop fusion | bytes 16515100 | tf_op jit(solution)/shard_map/jit(dynamic_index_in_dim)/squeeze | solution.py:78
  247.1 4.1 gather_fusion
  251.3 2.9 reshape.322
  254.2 3.6 fusion.203
  259.1 3.0 bitcast_dynamic-update-slice_fusion
  263.8 4.2 gather_fusion.1
  268.0 2.9 reshape.323
  271.0 4.7 fusion.202
  275.7 4.2 gather_fusion.2
  279.9 2.9 reshape.324
  282.9 4.7 fusion.201
  287.6 4.2 gather_fusion.3
  291.8 3.1 reshape.325
  294.9 4.7 fusion.200
  299.6 4.3 gather_fusion.4
  303.9 2.9 reshape.326
  308.0 2.7 fusion.50
  319.0 3.8 fusion.81
  324.1 3.0 fusion.199
  327.1 4.2 gather_fusion.5
  331.3 3.1 reshape.327
  337.2 2.7 fusion.51
  348.2 3.8 fusion.78
  353.2 2.9 fusion.198
  356.2 4.3 gather_fusion.6
  360.5 2.9 reshape.328
  364.8 2.7 fusion.52
  368.9 1.9 fusion.192
  375.8 3.6 fusion.75
  381.1 2.9 fusion.197
  384.1 1.9 fusion.8
  385.9 4.9 collective-permute-done.3
  392.7 2.1 fusion.53
  395.4 3.7 fusion.72
  400.8 8.6 %collective-permute-done.4 = bf16[48,4096]{1,0:T(8,128)(2,1)S(1)} collective-permute-done((bf16[48,4096]{1,0:T(8,128)(2,1)S(1)}, bf16[48,4096]{1,0:T(8,128)(2,1)S(1)}, u32[]{:S(2)}, u32[]{:S(2)}) %collective-permute-start.4) | collective-permute-done | bytes 393248 | tf_op jit(solution)/shard_map/ppermute | solution.py:10
  411.2 2.7 fusion.54
  421.9 3.6 fusion.69
  427.1 2.7 copy.377
  430.0 4.8 collective-permute-done.5
  436.6 2.7 fusion.55
  440.8 1.8 fusion.189
  447.6 1.9 fusion.3
  449.5 3.5 fusion.66
  453.1 174.1 %all-reduce.2.cloned.1.call-done = f32[1,4096,16]{1,2,0:T(8,128)} async-done(((f32[1,4096,16]{1,2,0:T(8,128)}), f32[1,4096,16]{1,2,0:T(8,128)}) %all-reduce.2.cloned.1.call-update) | async-done | bytes 262160 | tf_op jit(solution)/shard_map/psum | solution.py:94
  (254 shorter events, 100.8 us)
Async XLA Ops:
  7.2 20.7 %copy-start = (bf16[1,4,48,2,4096]{4,3,2,1,0:T(2,128)(2,1)S(1)}, bf16[1,4,48,2,4096]{4,3,2,1,0:T(2,128)(2,1)}, u32[]{:S(2)}) copy-start(bf16[1,4,48,2,4096]{4,3,2,1,0:T(2,128)(2,1)} %param.7) | copy-start | bytes 9437188
  13.7 10.1 %copy-start.43 = (s32[1,4,48,2]{2,3,1,0:T(2,128)S(1)}, s32[1,4,48,2]{2,3,1,0:T(2,128)}, u32[]{:S(2)}) copy-start(s32[1,4,48,2]{2,3,1,0:T(2,128)} %param.9) | copy-start | bytes 4612
  13.7 10.9 %copy-start.1 = (bf16[1,4096,16]{1,2,0:T(8,128)(2,1)S(1)}, bf16[1,4096,16]{1,2,0:T(8,128)(2,1)}, u32[]{:S(2)}) copy-start(bf16[1,4096,16]{1,2,0:T(8,128)(2,1)} %param.10) | copy-start | bytes 393220
  13.7 59.2 %all-to-all-start = ((bf16[1,16,9,4096]{3,2,0,1:T(8,128)(2,1)}), bf16[1,16,9,4096]{3,2,0,1:T(8,128)(2,1)}, u32[]{:S(2)}, u32[]{:S(2)}) async-start(bf16[1,16,9,4096]{3,2,0,1:T(8,128)(2,1)} %bitcast.551), calls=%async_computation | async-start | bytes 4194304 | tf_op jit(solution)/shard_map/all_to_all | solution.py:64
  26.8 3.3 copy-start.47
  34.2 38.7 %copy-start.41 = (s32[4,96]{1,0:T(4,128)}, s32[4,96]{1,0:T(4,128)S(1)}, u32[]{:S(2)}) copy-start(s32[4,96]{1,0:T(4,128)S(1)} %copy.75) | copy-start | bytes 4612
  34.3 38.6 %copy-start.20 = (s32[48,2]{1,0:T(8,128)}, s32[48,2]{1,0:T(8,128)S(1)}, u32[]{:S(2)}) copy-start(s32[48,2]{1,0:T(8,128)S(1)} %copy.79) | copy-start | bytes 1156
  35.5 0.6 copy-start.29
  36.2 41.6 %copy-start.18 = (s32[48,2]{1,0:T(8,128)}, s32[48,2]{1,0:T(8,128)S(1)}, u32[]{:S(2)}) copy-start(s32[48,2]{1,0:T(8,128)S(1)} %copy.82) | copy-start | bytes 1156
  72.9 54.0 %all-to-all-start.1 = ((bf16[1,16,9,4096]{3,2,0,1:T(8,128)(2,1)}), bf16[1,16,9,4096]{3,2,0,1:T(8,128)(2,1)}, u32[]{:S(2)}, u32[]{:S(2)}) async-start(bf16[1,16,9,4096]{3,2,0,1:T(8,128)(2,1)} %bitcast.550), calls=%async_computation.1 | async-start | bytes 4194304 | tf_op jit(solution)/shard_map/all_to_all | solution.py:64
  78.8 3.5 copy-start.7
  86.9 2.8 copy-start.19
  90.5 2.7 copy-start.16
  91.7 0.6 copy-start.23
  93.3 2.7 copy-start.15
  96.2 35.7 %copy-start.14 = (s32[48,2]{1,0:T(8,128)}, s32[48,2]{1,0:T(8,128)S(1)}, u32[]{:S(2)}) copy-start(s32[48,2]{1,0:T(8,128)S(1)} %copy.94) | copy-start | bytes 1156
  97.4 29.5 %copy-start.48 = (f32[48]{0:T(128)}, f32[48]{0:T(128)S(1)}, u32[]{:S(2)}) copy-start(f32[48]{0:T(128)S(1)} %get-tuple-element.93) | copy-start | bytes 580
  126.9 54.0 %all-to-all-start.2 = ((bf16[1,16,9,4096]{3,2,0,1:T(8,128)(2,1)}), bf16[1,16,9,4096]{3,2,0,1:T(8,128)(2,1)}, u32[]{:S(2)}, u32[]{:S(2)}) async-start(bf16[1,16,9,4096]{3,2,0,1:T(8,128)(2,1)} %bitcast.549), calls=%async_computation.2 | async-start | bytes 4194304 | tf_op jit(solution)/shard_map/all_to_all | solution.py:64
  132.2 54.2 %copy-start.44 = (f32[48,2]{0,1:T(2,128)}, f32[48,2]{0,1:T(2,128)S(1)}, u32[]{:S(2)}) copy-start(f32[48,2]{0,1:T(2,128)S(1)} %copy.167) | copy-start | bytes 1156
  180.9 6.0 copy-start.32
  181.0 6.0 copy-start.42
  181.0 6.0 copy-start.57
  181.0 6.0 copy-start.60
  181.0 54.2 %all-to-all-start.3 = ((bf16[1,16,9,4096]{3,2,0,1:T(8,128)(2,1)}), bf16[1,16,9,4096]{3,2,0,1:T(8,128)(2,1)}, u32[]{:S(2)}, u32[]{:S(2)}) async-start(bf16[1,16,9,4096]{3,2,0,1:T(8,128)(2,1)} %bitcast.548), calls=%async_computation.3 | async-start | bytes 4194304 | tf_op jit(solution)/shard_map/all_to_all | solution.py:64
  186.1 441.1 %all-reduce.2.cloned.1.call-start = ((), (), s32[]{:S(2)}) async-start(), calls=%async_computation.4 | async-start | bytes 524288 | tf_op jit(solution)/shard_map/psum | solution.py:94
  196.1 2.5 copy-start.9
  198.6 1.7 copy-start.8
  257.8 1.4 copy-start.61
  257.8 1.4 copy-start.62
  262.1 44.7 %collective-permute-start = (bf16[48,4096]{1,0:T(8,128)(2,1)}, bf16[48,4096]{1,0:T(8,128)(2,1)}, u32[]{:S(2)}, u32[]{:S(2)}) collective-permute-start(bf16[48,4096]{1,0:T(8,128)(2,1)} %get-tuple-element.72), channel_id=1, source_target_pairs={{64,0},{128,64},{192,128},{65,1},{129,65},{193,129},{66,2},{130,66... | collective-permute-start | bytes 1179656 | tf_op jit(solution)/shard_map/ppermute | solution.py:10
  308.0 10.3 %copy-start.30 = (f32[48,16]{0,1:T(8,128)S(1)}, f32[48,16]{0,1:T(8,128)}, u32[]{:S(2)}) copy-start(f32[48,16]{0,1:T(8,128)} %copy-done.29) | copy-start | bytes 9220
  319.0 3.8 copy-start.33
  319.0 5.1 copy-start.4
  322.8 13.2 %collective-permute-start.1 = (bf16[48,4096]{1,0:T(8,128)(2,1)}, bf16[48,4096]{1,0:T(8,128)(2,1)}, u32[]{:S(2)}, u32[]{:S(2)}) collective-permute-start(bf16[48,4096]{1,0:T(8,128)(2,1)} %get-tuple-element.76), channel_id=1, source_target_pairs={{64,0},{128,64},{192,128},{65,1},{129,65},{193,129},{66,2},{130,66... | collective-permute-start | bytes 1179656 | tf_op jit(solution)/shard_map/ppermute | solution.py:10
  337.1 10.3 %copy-start.26 = (f32[48,16]{0,1:T(8,128)S(1)}, f32[48,16]{0,1:T(8,128)}, u32[]{:S(2)}) copy-start(f32[48,16]{0,1:T(8,128)} %copy-done.25) | copy-start | bytes 9220
  348.2 3.8 copy-start.35
  348.2 5.1 copy-start.5
  352.0 11.6 %collective-permute-start.2 = (bf16[48,4096]{1,0:T(8,128)(2,1)}, bf16[48,4096]{1,0:T(8,128)(2,1)}, u32[]{:S(2)}, u32[]{:S(2)}) collective-permute-start(bf16[48,4096]{1,0:T(8,128)(2,1)} %get-tuple-element.80), channel_id=1, source_target_pairs={{64,0},{128,64},{192,128},{65,1},{129,65},{193,129},{66,2},{130,66... | collective-permute-start | bytes 1179656 | tf_op jit(solution)/shard_map/ppermute | solution.py:10
  364.7 10.3 %copy-start.28 = (f32[48,16]{0,1:T(8,128)S(1)}, f32[48,16]{0,1:T(8,128)}, u32[]{:S(2)}) copy-start(f32[48,16]{0,1:T(8,128)} %copy-done.27) | copy-start | bytes 9220
  375.8 3.7 copy-start.37
  375.8 5.3 copy-start.6
  379.4 4.6 copy-start.34
  379.4 11.4 %collective-permute-start.3 = (bf16[48,4096]{1,0:T(8,128)(2,1)S(1)}, bf16[48,4096]{1,0:T(8,128)(2,1)S(1)}, u32[]{:S(2)}, u32[]{:S(2)}) collective-permute-start(bf16[48,4096]{1,0:T(8,128)(2,1)S(1)} %get-tuple-element.84), channel_id=1, source_target_pairs={{64,0},{128,64},{192,128},{65,1},{129,65},{193,129},{66,2},{130,66... | collective-permute-start | bytes 1179656 | tf_op jit(solution)/shard_map/ppermute | solution.py:10
  390.8 0.7 copy-start.12
  392.6 2.3 copy-start.46
  392.6 2.4 copy-start.17
  392.7 2.6 copy-start.24
  392.7 2.6 copy-start.52
  392.7 2.7 copy-start.58
  392.7 2.7 copy-start.59
  395.3 3.7 copy-start.39
  395.3 5.0 copy-start.2
  395.4 5.0 copy-start.13
  395.4 5.0 copy-start.36
  395.4 5.2 copy-start.38
  399.1 10.3 %collective-permute-start.4 = (bf16[48,4096]{1,0:T(8,128)(2,1)S(1)}, bf16[48,4096]{1,0:T(8,128)(2,1)S(1)}, u32[]{:S(2)}, u32[]{:S(2)}) collective-permute-start(bf16[48,4096]{1,0:T(8,128)(2,1)S(1)} %get-tuple-element.88), channel_id=1, source_target_pairs={{64,0},{128,64},{192,128},{65,1},{129,65},{193,129},{66,2},{130,66... | collective-permute-start | bytes 1179656 | tf_op jit(solution)/shard_map/ppermute | solution.py:10
  409.4 0.7 copy-start.11
  411.2 10.1 %copy-start.22 = (f32[48,16]{0,1:T(8,128)S(1)}, f32[48,16]{0,1:T(8,128)}, u32[]{:S(2)}) copy-start(f32[48,16]{0,1:T(8,128)} %copy-done.21) | copy-start | bytes 9220
  421.9 4.9 copy-start.3
  421.9 5.0 copy-start.40
  425.6 9.2 %collective-permute-start.5 = (bf16[48,4096]{1,0:T(8,128)(2,1)S(1)}, bf16[48,4096]{1,0:T(8,128)(2,1)S(1)}, u32[]{:S(2)}, u32[]{:S(2)}) collective-permute-start(bf16[48,4096]{1,0:T(8,128)(2,1)S(1)} %get-tuple-element.92), channel_id=1, source_target_pairs={{64,0},{128,64},{192,128},{65,1},{129,65},{193,129},{66,2},{130,66... | collective-permute-start | bytes 1179656 | tf_op jit(solution)/shard_map/ppermute | solution.py:10
  434.8 0.8 copy-start.10
  436.6 4.2 copy-start.45
  436.6 10.3 %copy-start.49 = (f32[48]{0:T(128)S(1)}, f32[48]{0:T(128)}, u32[]{:S(2)}) copy-start(f32[48]{0:T(128)} %copy-done.48) | copy-start | bytes 580
  (10 other events, 6.0 us)
Sparse Core Ops, SparseCore 0:
  449.7 177.4 all-reduce.1
where the time goes:
time: 646 us; the launch traced here: 636 us
  waiting for transfers between devices  328 us (51%)
  local copies, waits for them, and re-layouts  165 us (26%)
  matrix products  57.4 us (9%)
  other arithmetic  35.6 us (6%)
  starting transfers between devices  33.9 us (5%)
  between operations  15.2 us (2%)
    psum x1, waiting for transfers between devices, on_device(): router_grad = lax.psum(weight_sum / micro, ('expert', 'dp'))  174 us
    all_to_all x4, waiting for transfers between devices, on_device(): lax.all_to_all(local_grads[block_num], 'expert', split_axis=1, concat_axi...  134 us
    unnamed x150, local copies, waits for them, and re-layouts  34.3 us
    gather x7, local copies, waits for them, and re-layouts, block_grad(): returned[index_rows].reshape(rows_dev, 2, width).astype(jnp.float32)  29.6 us
    slice x7, local copies, waits for them, and re-layouts, block_grad(): back_rows[:, 0]  26.5 us
    all_to_all x4, starting transfers between devices, on_device(): lax.all_to_all(local_grads[block_num], 'expert', split_axis=1, concat_axi...  25.2 us
    dot_general x7, matrix products, block_grad(): lax.dot_general(dense, router_w, (((1,), (1,)), ((), ())), preferred_elem...  25 us
    convert_element_type x7, local copies, waits for them, and re-layouts, block_grad(): returned[index_rows].reshape(rows_dev, 2, width).astype(jnp.float32)  20.9 us
  transfers between devices with their start and end apart: 11, of which 10 were waited for; matrix products, arithmetic and copies ran while one was open for 21% of the time, Pallas kernels for 0%

commit v1 on v0

--- a/solution.py
+++ b/solution.py
@@ -91,7 +91,7 @@
         grad_buffer = jnp.where(is_active, updated, grad_buffer)
         weight_sum = weight_sum + jnp.where(is_active, weight_part, 0.0)
         passed = new_grad
-    router_grad = lax.psum(weight_sum / micro, ("expert", "dp"))
+    router_grad = lax.psum(lax.psum(weight_sum / micro, "expert"), "dp")
     return (grad_buffer[None], router_grad[None])
 
 

time: 646 us -> 619 us (0.958)
  waiting for transfers between devices: 328 us -> 301 us
    psum x1 -> x2, waiting for transfers between devices: 174 us -> 147 us  [on_device(): router_grad = lax.psum(lax.psum(weight_sum / micro, 'expert'), 'dp')]
    unnamed x150 -> x152, local copies, waits for them, and re-layouts: 34.3 us -> 33.4 us
  transfers between devices with their start and end apart: 11 -> 12, of which waited for: 10 -> 10; matrix products, arithmetic and copies ran while one was open for 21% -> 22% of each run, Pallas kernels for 0% -> 0%
where the time goes in v1:
time: 619 us; the launch traced here: 608 us
  waiting for transfers between devices  301 us (49%)
  local copies, waits for them, and re-layouts  164 us (26%)
  matrix products  57.5 us (9%)
  other arithmetic  35.8 us (6%)
  starting transfers between devices  33.8 us (5%)
  between operations  15.3 us (2%)
    psum x2, waiting for transfers between devices, on_device(): router_grad = lax.psum(lax.psum(weight_sum / micro, 'expert'), 'dp')  147 us
    all_to_all x4, waiting for transfers between devices, on_device(): lax.all_to_all(local_grads[block_num], 'expert', split_axis=1, concat_axi...  134 us
    unnamed x152, local copies, waits for them, and re-layouts  33.4 us
    gather x7, local copies, waits for them, and re-layouts, block_grad(): returned[index_rows].reshape(rows_dev, 2, width).astype(jnp.float32)  29.5 us
    slice x7, local copies, waits for them, and re-layouts, block_grad(): back_rows[:, 0]  26.5 us
    all_to_all x4, starting transfers between devices, on_device(): lax.all_to_all(local_grads[block_num], 'expert', split_axis=1, concat_axi...  25.2 us
    dot_general x7, matrix products, block_grad(): lax.dot_general(dense, router_w, (((1,), (1,)), ((), ())), preferred_elem...  25.1 us
    convert_element_type x7, local copies, waits for them, and re-layouts, block_grad(): returned[index_rows].reshape(rows_dev, 2, width).astype(jnp.float32)  20.9 us
  transfers between devices with their start and end apart: 12, of which 10 were waited for; matrix products, arithmetic and copies ran while one was open for 22% of the time, Pallas kernels for 0%

profile of v1, /device:TPU:1, one launch (start us, length us, event | category | flops | bytes accessed | tf_op | source)
XLA Modules:
  0.0 608.1 jit_solution(5254150858016762186)
XLA Ops:
  7.2 4.4 fusion.195
  11.6 2.1 copy.367
  13.7 10.1 %all-to-all-start = ((bf16[1,16,9,4096]{3,2,0,1:T(8,128)(2,1)}), bf16[1,16,9,4096]{3,2,0,1:T(8,128)(2,1)}, u32[]{:S(2)}, u32[]{:S(2)}) async-start(bf16[1,16,9,4096]{3,2,0,1:T(8,128)(2,1)} %bitcast.550), calls=%async_computation | async-start | bytes 4194304 | tf_op jit(solution)/shard_map/all_to_all | solution.py:64
  27.8 2.1 fusion.48
  30.7 3.4 copy.366
  39.3 33.5 %all-to-all-done = bf16[1,16,9,4096]{3,2,0,1:T(8,128)(2,1)} async-done(((bf16[1,16,9,4096]{3,2,0,1:T(8,128)(2,1)}), bf16[1,16,9,4096]{3,2,0,1:T(8,128)(2,1)}, u32[]{:S(2)}, u32[]{:S(2)}) %all-to-all-start) | async-done | bytes 1179680 | tf_op jit(solution)/shard_map/all_to_all | solution.py:64
  72.9 5.0 all-to-all-start.1
  78.7 3.5 copy.365
  82.3 2.1 copy.364
  97.5 29.4 %all-to-all-done.1 = bf16[1,16,9,4096]{3,2,0,1:T(8,128)(2,1)} async-done(((bf16[1,16,9,4096]{3,2,0,1:T(8,128)(2,1)}), bf16[1,16,9,4096]{3,2,0,1:T(8,128)(2,1)}, u32[]{:S(2)}, u32[]{:S(2)}) %all-to-all-start.1) | async-done | bytes 1179680 | tf_op jit(solution)/shard_map/all_to_all | solution.py:64
  126.9 5.0 all-to-all-start.2
  143.5 37.5 %all-to-all-done.2 = bf16[1,16,9,4096]{3,2,0,1:T(8,128)(2,1)} async-done(((bf16[1,16,9,4096]{3,2,0,1:T(8,128)(2,1)}), bf16[1,16,9,4096]{3,2,0,1:T(8,128)(2,1)}, u32[]{:S(2)}, u32[]{:S(2)}) %all-to-all-start.2) | async-done | bytes 1179680 | tf_op jit(solution)/shard_map/all_to_all | solution.py:64
  180.9 5.1 all-to-all-start.3
  188.1 2.6 stack_reshape.12
  190.7 2.6 stack_reshape.13
  193.4 2.6 stack_reshape.14
  196.0 2.5 constant_dynamic-update-slice_fusion.3
  201.3 33.8 %all-to-all-done.3 = bf16[1,16,9,4096]{3,2,0,1:T(8,128)(2,1)} async-done(((bf16[1,16,9,4096]{3,2,0,1:T(8,128)(2,1)}), bf16[1,16,9,4096]{3,2,0,1:T(8,128)(2,1)}, u32[]{:S(2)}, u32[]{:S(2)}) %all-to-all-start.3) | async-done | bytes 1179680 | tf_op jit(solution)/shard_map/all_to_all | solution.py:64
  235.1 2.6 stack_reshape.15
  237.7 2.4 constant_dynamic-update-slice_fusion
  240.1 7.0 %dynamic-slice_bitcast_fusion = (bf16[144,4096]{1,0:T(8,128)(2,1)}, bf16[144,4096]{1,0:T(8,128)(2,1)}, bf16[144,4096]{1,0:T(8,128)(2,1)}, bf16[144,4096]{1,0:T(8...) fusion(bf16[4,144,4096]{2,1,0:T(8,128)(2,1)} %constant_dynamic-update-slice_fusion, ...), kind=kLoop, calls=%fused_computation.27 | loop fusion | bytes 16515100 | tf_op jit(solution)/shard_map/jit(dynamic_index_in_dim)/squeeze | solution.py:78
  247.1 4.1 gather_fusion
  251.2 2.9 reshape.322
  254.2 3.6 fusion.202
  259.1 3.0 bitcast_dynamic-update-slice_fusion
  263.8 4.2 gather_fusion.1
  268.0 2.9 reshape.323
  271.0 4.7 fusion.201
  275.7 4.2 gather_fusion.2
  279.9 2.9 reshape.324
  282.9 4.7 fusion.200
  287.6 4.2 gather_fusion.3
  291.8 3.1 reshape.325
  296.1 2.7 fusion.49
  307.0 3.8 fusion.80
  312.1 3.0 fusion.199
  315.1 4.3 gather_fusion.4
  319.4 2.9 reshape.326
  325.2 2.7 fusion.50
  329.3 1.9 fusion.192
  336.2 3.8 fusion.77
  341.3 2.9 fusion.198
  344.2 4.2 gather_fusion.5
  348.5 3.1 reshape.327
  352.8 2.7 fusion.51
  357.0 1.8 fusion.191
  363.8 3.8 fusion.74
  368.9 3.0 fusion.197
  371.9 4.2 gather_fusion.6
  376.1 2.9 reshape.328
  379.0 1.9 fusion.7
  382.1 2.1 fusion.52
  384.8 3.6 fusion.71
  390.4 10.2 %collective-permute-done.4 = bf16[48,4096]{1,0:T(8,128)(2,1)S(1)} collective-permute-done((bf16[48,4096]{1,0:T(8,128)(2,1)S(1)}, bf16[48,4096]{1,0:T(8,128)(2,1)S(1)}, u32[]{:S(2)}, u32[]{:S(2)}) %collective-permute-start.4) | collective-permute-done | bytes 393248 | tf_op jit(solution)/shard_map/ppermute | solution.py:10
  402.4 2.7 fusion.53
  413.3 3.6 fusion.68
  418.6 8.4 %collective-permute-done.5 = bf16[48,4096]{1,0:T(8,128)(2,1)S(1)} collective-permute-done((bf16[48,4096]{1,0:T(8,128)(2,1)S(1)}, bf16[48,4096]{1,0:T(8,128)(2,1)S(1)}, u32[]{:S(2)}, u32[]{:S(2)}) %collective-permute-start.5) | collective-permute-done | bytes 393248 | tf_op jit(solution)/shard_map/ppermute | solution.py:10
  428.8 2.7 fusion.54
  439.6 1.9 fusion.2
  441.5 4.7 fusion.196
  446.2 2.7 copy.377
  448.9 102.8 %all-reduce.3.cloned.1.call-done = f32[4096,16]{0,1:T(8,128)} async-done(((f32[4096,16]{0,1:T(8,128)}), f32[4096,16]{0,1:T(8,128)}) %all-reduce.3.cloned.1.call-update) | async-done | bytes 262160 | tf_op jit(solution)/shard_map/psum | solution.py:94
  551.8 3.5 fusion.65
  555.3 43.9 %all-reduce.5.cloned.1.call-done = f32[1,4096,16]{1,2,0:T(8,128)} async-done(((f32[1,4096,16]{1,2,0:T(8,128)}), f32[1,4096,16]{1,2,0:T(8,128)}) %all-reduce.5.cloned.1.call-update) | async-done | bytes 262160 | tf_op jit(solution)/shard_map/psum | solution.py:94
  (259 shorter events, 100.2 us)
Async XLA Ops:
  7.2 20.6 %copy-start = (bf16[1,4,48,2,4096]{4,3,2,1,0:T(2,128)(2,1)S(1)}, bf16[1,4,48,2,4096]{4,3,2,1,0:T(2,128)(2,1)}, u32[]{:S(2)}) copy-start(bf16[1,4,48,2,4096]{4,3,2,1,0:T(2,128)(2,1)} %param.7) | copy-start | bytes 9437188
  13.7 10.1 %copy-start.42 = (s32[1,4,48,2]{2,3,1,0:T(2,128)S(1)}, s32[1,4,48,2]{2,3,1,0:T(2,128)}, u32[]{:S(2)}) copy-start(s32[1,4,48,2]{2,3,1,0:T(2,128)} %param.9) | copy-start | bytes 4612
  13.7 10.9 %copy-start.1 = (bf16[1,4096,16]{1,2,0:T(8,128)(2,1)S(1)}, bf16[1,4096,16]{1,2,0:T(8,128)(2,1)}, u32[]{:S(2)}) copy-start(bf16[1,4096,16]{1,2,0:T(8,128)(2,1)} %param.10) | copy-start | bytes 393220
  13.7 59.2 %all-to-all-start = ((bf16[1,16,9,4096]{3,2,0,1:T(8,128)(2,1)}), bf16[1,16,9,4096]{3,2,0,1:T(8,128)(2,1)}, u32[]{:S(2)}, u32[]{:S(2)}) async-start(bf16[1,16,9,4096]{3,2,0,1:T(8,128)(2,1)} %bitcast.550), calls=%async_computation | async-start | bytes 4194304 | tf_op jit(solution)/shard_map/all_to_all | solution.py:64
  26.8 3.3 copy-start.46
  34.1 38.7 %copy-start.40 = (s32[4,96]{1,0:T(4,128)}, s32[4,96]{1,0:T(4,128)S(1)}, u32[]{:S(2)}) copy-start(s32[4,96]{1,0:T(4,128)S(1)} %copy.75) | copy-start | bytes 4612
  34.2 38.6 %copy-start.19 = (s32[48,2]{1,0:T(8,128)}, s32[48,2]{1,0:T(8,128)S(1)}, u32[]{:S(2)}) copy-start(s32[48,2]{1,0:T(8,128)S(1)} %copy.79) | copy-start | bytes 1156
  36.2 41.6 %copy-start.17 = (s32[48,2]{1,0:T(8,128)}, s32[48,2]{1,0:T(8,128)S(1)}, u32[]{:S(2)}) copy-start(s32[48,2]{1,0:T(8,128)S(1)} %copy.82) | copy-start | bytes 1156
  72.9 54.0 %all-to-all-start.1 = ((bf16[1,16,9,4096]{3,2,0,1:T(8,128)(2,1)}), bf16[1,16,9,4096]{3,2,0,1:T(8,128)(2,1)}, u32[]{:S(2)}, u32[]{:S(2)}) async-start(bf16[1,16,9,4096]{3,2,0,1:T(8,128)(2,1)} %bitcast.549), calls=%async_computation.1 | async-start | bytes 4194304 | tf_op jit(solution)/shard_map/all_to_all | solution.py:64
  78.7 3.5 copy-start.7
  86.9 2.8 copy-start.18
  90.4 2.8 copy-start.15
  93.3 2.8 copy-start.14
  96.2 35.7 %copy-start.13 = (s32[48,2]{1,0:T(8,128)}, s32[48,2]{1,0:T(8,128)S(1)}, u32[]{:S(2)}) copy-start(s32[48,2]{1,0:T(8,128)S(1)} %copy.94) | copy-start | bytes 1156
  97.4 29.5 %copy-start.47 = (f32[48]{0:T(128)}, f32[48]{0:T(128)S(1)}, u32[]{:S(2)}) copy-start(f32[48]{0:T(128)S(1)} %get-tuple-element.93) | copy-start | bytes 580
  126.9 54.0 %all-to-all-start.2 = ((bf16[1,16,9,4096]{3,2,0,1:T(8,128)(2,1)}), bf16[1,16,9,4096]{3,2,0,1:T(8,128)(2,1)}, u32[]{:S(2)}, u32[]{:S(2)}) async-start(bf16[1,16,9,4096]{3,2,0,1:T(8,128)(2,1)} %bitcast.548), calls=%async_computation.2 | async-start | bytes 4194304 | tf_op jit(solution)/shard_map/all_to_all | solution.py:64
  132.2 54.2 %copy-start.43 = (f32[48,2]{0,1:T(2,128)}, f32[48,2]{0,1:T(2,128)S(1)}, u32[]{:S(2)}) copy-start(f32[48,2]{0,1:T(2,128)S(1)} %copy.167) | copy-start | bytes 1156
  180.9 6.0 copy-start.31
  180.9 6.0 copy-start.41
  180.9 6.0 copy-start.56
  180.9 6.0 copy-start.61
  180.9 54.2 %all-to-all-start.3 = ((bf16[1,16,9,4096]{3,2,0,1:T(8,128)(2,1)}), bf16[1,16,9,4096]{3,2,0,1:T(8,128)(2,1)}, u32[]{:S(2)}, u32[]{:S(2)}) async-start(bf16[1,16,9,4096]{3,2,0,1:T(8,128)(2,1)} %bitcast.547), calls=%async_computation.3 | async-start | bytes 4194304 | tf_op jit(solution)/shard_map/all_to_all | solution.py:64
  186.1 365.7 %all-reduce.3.cloned.1.call-start = ((), (), s32[]{:S(2)}) async-start(), calls=%async_computation.4 | async-start | bytes 524288 | tf_op jit(solution)/shard_map/psum | solution.py:94
  196.0 2.5 copy-start.9
  198.5 1.7 copy-start.8
  257.7 1.4 copy-start.62
  257.7 1.4 copy-start.63
  262.1 32.8 %collective-permute-start = (bf16[48,4096]{1,0:T(8,128)(2,1)}, bf16[48,4096]{1,0:T(8,128)(2,1)}, u32[]{:S(2)}, u32[]{:S(2)}) collective-permute-start(bf16[48,4096]{1,0:T(8,128)(2,1)} %get-tuple-element.72), channel_id=1, source_target_pairs={{64,0},{128,64},{192,128},{65,1},{129,65},{193,129},{66,2},{130,66... | collective-permute-start | bytes 1179656 | tf_op jit(solution)/shard_map/ppermute | solution.py:10
  296.0 10.3 %copy-start.29 = (f32[48,16]{0,1:T(8,128)S(1)}, f32[48,16]{0,1:T(8,128)}, u32[]{:S(2)}) copy-start(f32[48,16]{0,1:T(8,128)} %copy-done.28) | copy-start | bytes 9220
  307.0 3.8 copy-start.32
  307.0 5.1 copy-start.4
  310.8 13.2 %collective-permute-start.1 = (bf16[48,4096]{1,0:T(8,128)(2,1)}, bf16[48,4096]{1,0:T(8,128)(2,1)}, u32[]{:S(2)}, u32[]{:S(2)}) collective-permute-start(bf16[48,4096]{1,0:T(8,128)(2,1)} %get-tuple-element.76), channel_id=1, source_target_pairs={{64,0},{128,64},{192,128},{65,1},{129,65},{193,129},{66,2},{130,66... | collective-permute-start | bytes 1179656 | tf_op jit(solution)/shard_map/ppermute | solution.py:10
  325.2 10.3 %copy-start.25 = (f32[48,16]{0,1:T(8,128)S(1)}, f32[48,16]{0,1:T(8,128)}, u32[]{:S(2)}) copy-start(f32[48,16]{0,1:T(8,128)} %copy-done.24) | copy-start | bytes 9220
  336.2 3.8 copy-start.34
  336.2 5.1 copy-start.5
  340.0 11.7 %collective-permute-start.2 = (bf16[48,4096]{1,0:T(8,128)(2,1)}, bf16[48,4096]{1,0:T(8,128)(2,1)}, u32[]{:S(2)}, u32[]{:S(2)}) collective-permute-start(bf16[48,4096]{1,0:T(8,128)(2,1)} %get-tuple-element.80), channel_id=1, source_target_pairs={{64,0},{128,64},{192,128},{65,1},{129,65},{193,129},{66,2},{130,66... | collective-permute-start | bytes 1179656 | tf_op jit(solution)/shard_map/ppermute | solution.py:10
  352.8 10.3 %copy-start.27 = (f32[48,16]{0,1:T(8,128)S(1)}, f32[48,16]{0,1:T(8,128)}, u32[]{:S(2)}) copy-start(f32[48,16]{0,1:T(8,128)} %copy-done.26) | copy-start | bytes 9220
  363.8 3.8 copy-start.36
  363.8 5.1 copy-start.6
  367.6 13.3 %collective-permute-start.3 = (bf16[48,4096]{1,0:T(8,128)(2,1)}, bf16[48,4096]{1,0:T(8,128)(2,1)}, u32[]{:S(2)}, u32[]{:S(2)}) collective-permute-start(bf16[48,4096]{1,0:T(8,128)(2,1)} %get-tuple-element.84), channel_id=1, source_target_pairs={{64,0},{128,64},{192,128},{65,1},{129,65},{193,129},{66,2},{130,66... | collective-permute-start | bytes 1179656 | tf_op jit(solution)/shard_map/ppermute | solution.py:10
  376.1 2.9 copy-start.33
  382.1 2.3 copy-start.45
  382.1 2.4 copy-start.16
  382.1 2.6 copy-start.23
  382.1 2.6 copy-start.51
  382.1 2.7 copy-start.59
  382.1 2.7 copy-start.60
  384.7 3.7 copy-start.38
  384.8 5.2 copy-start.2
  384.8 5.2 copy-start.12
  384.8 5.2 copy-start.35
  384.8 5.4 copy-start.37
  388.5 12.1 %collective-permute-start.4 = (bf16[48,4096]{1,0:T(8,128)(2,1)S(1)}, bf16[48,4096]{1,0:T(8,128)(2,1)S(1)}, u32[]{:S(2)}, u32[]{:S(2)}) collective-permute-start(bf16[48,4096]{1,0:T(8,128)(2,1)S(1)} %get-tuple-element.88), channel_id=1, source_target_pairs={{64,0},{128,64},{192,128},{65,1},{129,65},{193,129},{66,2},{130,66... | collective-permute-start | bytes 1179656 | tf_op jit(solution)/shard_map/ppermute | solution.py:10
  400.6 0.8 copy-start.11
  402.4 10.1 %copy-start.21 = (f32[48,16]{0,1:T(8,128)S(1)}, f32[48,16]{0,1:T(8,128)}, u32[]{:S(2)}) copy-start(f32[48,16]{0,1:T(8,128)} %copy-done.20) | copy-start | bytes 9220
  413.3 4.9 copy-start.3
  413.3 5.0 copy-start.39
  416.9 10.0 %collective-permute-start.5 = (bf16[48,4096]{1,0:T(8,128)(2,1)S(1)}, bf16[48,4096]{1,0:T(8,128)(2,1)S(1)}, u32[]{:S(2)}, u32[]{:S(2)}) collective-permute-start(bf16[48,4096]{1,0:T(8,128)(2,1)S(1)} %get-tuple-element.92), channel_id=1, source_target_pairs={{64,0},{128,64},{192,128},{65,1},{129,65},{193,129},{66,2},{130,66... | collective-permute-start | bytes 1179656 | tf_op jit(solution)/shard_map/ppermute | solution.py:10
  427.0 0.7 copy-start.10
  428.8 4.1 copy-start.44
  428.8 10.1 %copy-start.48 = (f32[48]{0:T(128)S(1)}, f32[48]{0:T(128)}, u32[]{:S(2)}) copy-start(f32[48]{0:T(128)} %copy-done.47) | copy-start | bytes 580
  441.5 157.7 %all-reduce.5.cloned.1.call-start = ((), (), s32[]{:S(2)}) async-start(), calls=%async_computation.5 | async-start | bytes 524288 | tf_op jit(solution)/shard_map/psum | solution.py:94
  446.2 105.5 %copy-start.57 = (f32[48]{0:T(128)S(1)}, f32[48]{0:T(128)}, u32[]{:S(2)}) copy-start(f32[48]{0:T(128)} %get-tuple-element.55) | copy-start | bytes 580
  446.2 105.5 %copy-start.58 = (f32[48]{0:T(128)S(1)}, f32[48]{0:T(128)}, u32[]{:S(2)}) copy-start(f32[48]{0:T(128)} %get-tuple-element.56) | copy-start | bytes 580
  (12 other events, 7.2 us)
Sparse Core Ops, SparseCore 0:
  441.6 110.0 all-reduce.2
  554.2 44.9 all-reduce.4
